TPU v7x, 32 devices: a whole 2x2x4 slice. The times are simulated.
32 devices in a mesh: blk: 16 (over z, y, core), tp: 2 (over x).
Axes of the slice: x: 2, y: 2, z: 4, core: 2. Of those that a mesh axis runs over, the one named last changes fastest.
Arguments:
- frames: bfloat16 [4096, 1024], P('blk'), may hold values from -6 to 6
- clip_lengths: int32 [8], replicated, may hold values from 1 to 3841, 4096 in all
- text_states: bfloat16 [128, 1024], replicated, may hold values from -6 to 6
- text_segments: int32 [128], replicated, may hold values from 0 to 7, never falling along the last dimension, each value on 1 to 32 neighbouring positions
- gain_one: float32 [1024], replicated, may hold values from 0.1 to 1.9
- shift_one: float32 [1024], replicated, may hold values from -1.5 to 1.5
- gain_two: float32 [1024], replicated, may hold values from 0.1 to 1.9
- shift_two: float32 [1024], replicated, may hold values from -1.5 to 1.5
- gain_three: float32 [1024], replicated, may hold values from 0.1 to 1.9
- shift_three: float32 [1024], replicated, may hold values from -1.5 to 1.5
- query_weight: bfloat16 [1024, 1024], P(None, 'tp'), may hold values from -0.1875 to 0.1875
- key_weight: bfloat16 [1024, 1024], P(None, 'tp'), may hold values from -0.1875 to 0.1875
- value_weight: bfloat16 [1024, 1024], P(None, 'tp'), may hold values from -0.1875 to 0.1875
- output_weight: bfloat16 [1024, 1024], P('tp'), may hold values from -0.75 to 0.75
- cross_query: bfloat16 [1024, 1024], P(None, 'tp'), may hold values from -0.1875 to 0.1875
- cross_key: bfloat16 [1024, 1024], P(None, 'tp'), may hold values from -0.1875 to 0.1875
- cross_value: bfloat16 [1024, 1024], P(None, 'tp'), may hold values from -0.1875 to 0.1875
- cross_output: bfloat16 [1024, 1024], P('tp'), may hold values from -0.375 to 0.375
- inner_weight: bfloat16 [1024, 4096], P(None, 'tp'), may hold values from -0.1875 to 0.1875
- outer_weight: bfloat16 [4096, 1024], P('tp'), may hold values from -0.09375 to 0.09375
- cotangent: bfloat16 [4096, 1024], P('blk'), may hold values from -6 to 6
Outputs:
- result: bfloat16 [4096, 1024], P('blk')
- grad_frames: bfloat16 [4096, 1024], P('blk')
- grad_text: float32 [128, 1024], replicated
- grad_gain_one: float32 [1024], replicated
- grad_shift_one: float32 [1024], replicated
- grad_gain_two: float32 [1024], replicated
- grad_shift_two: float32 [1024], replicated
- grad_gain_three: float32 [1024], replicated
- grad_shift_three: float32 [1024], replicated
- grad_query_weight: float32 [1024, 1024], P(None, 'tp')
- grad_key_weight: float32 [1024, 1024], P(None, 'tp')
- grad_value_weight: float32 [1024, 1024], P(None, 'tp')
- grad_output_weight: float32 [1024, 1024], P('tp')
- grad_cross_query: float32 [1024, 1024], P(None, 'tp')
- grad_cross_key: float32 [1024, 1024], P(None, 'tp')
- grad_cross_value: float32 [1024, 1024], P(None, 'tp')
- grad_cross_output: float32 [1024, 1024], P('tp')
- grad_inner_weight: float32 [1024, 4096], P(None, 'tp')
- grad_outer_weight: float32 [4096, 1024], P('tp')
Inputs may be any that keep to these rules, and one draw needn't show every extreme that they name: `clip_lengths`: clips follow one another in the pack; one of them has 3841 frames. `text_segments`: text tokens of a clip stand together and in clip order; every clip has 1 to 32 of them, one exactly 32.
All inputs are finite; a program needn't handle non-finite values.
Results may differ from a plain program's by a relative error of at most 0.028.
Values may be sent and summed in bfloat16 or wider, within the bound.
No kernel may reach another device: no remote copies, remote signals or barrier semaphores. Data moves between devices by JAX's collectives and lax.ppermute only.
A program may use at most 384 MiB of HBM per device.

v0:
```python
import jax
import jax.numpy as jnp
from jax import lax
from jax.sharding import PartitionSpec as P

HEAD_DIM = 64
EPSILON = 1e-05
NEGATIVE = -1e30


def shifted(block, axis, distance):
    devices = range(lax.axis_size(axis))
    route = [(i - distance, i) for i in devices if i - distance in devices]
    return lax.ppermute(block, axis, route)


def shifted_2(value, axis, by):
    size = lax.axis_size(axis)
    return lax.ppermute(value, axis, [(i, (i + by) % size) for i in range(size)])


def layer_norm(values, gain, shift):
    centre = values - jnp.mean(values, axis=-1, keepdims=True)
    spread = jnp.mean(centre * centre, axis=-1, keepdims=True)
    return centre * lax.rsqrt(spread + EPSILON) * gain + shift


def norm_grads(values, gain, shift, grad):
    _, pullback = jax.vjp(layer_norm, values, gain, shift)
    return pullback(grad)


def gelu_exact(values):
    return jax.nn.gelu(values, approximate=False)


def clip_rows(positions, clip_lengths):
    ends = jnp.cumsum(clip_lengths)
    starts = ends - clip_lengths
    segment = jnp.sum((positions[:, None] >= ends[None, :]).astype(jnp.int32), axis=1)
    match = segment[:, None] == jnp.arange(clip_lengths.shape[0], dtype=jnp.int32)[None, :]
    first = jnp.sum(jnp.where(match, starts[None, :], 0), axis=1)
    return (segment, first)


def matmul(left, right):
    return jnp.dot(left, right, preferred_element_type=jnp.float32)


def head_sum(values):
    return lax.psum(values.astype(jnp.bfloat16), "tp").astype(jnp.float32)


def unchanged(state):
    return state


def block_grads(
    query_heads,
    grad_heads,
    log_total,
    delta,
    query_rows,
    query_first,
    key_heads,
    value_heads,
    key_rows,
):
    allowed = (key_rows[None, :] <= query_rows[:, None]) & (
        key_rows[None, :] >= query_first[:, None]
    )
    score = jnp.einsum("qhd,khd->hqk", query_heads, key_heads, preferred_element_type=jnp.float32)
    weights = jnp.exp(jnp.where(allowed[None], score - log_total[:, :, None], NEGATIVE))
    grad_weights = jnp.einsum(
        "qhd,khd->hqk", grad_heads, value_heads, preferred_element_type=jnp.float32
    )
    grad_score = (weights * (grad_weights - delta[:, :, None])).astype(jnp.bfloat16)
    query_part = jnp.einsum(
        "hqk,khd->qhd", grad_score, key_heads, preferred_element_type=jnp.float32
    )
    key_part = jnp.einsum(
        "hqk,qhd->khd", grad_score, query_heads, preferred_element_type=jnp.float32
    )
    value_part = jnp.einsum(
        "hqk,qhd->khd", weights.astype(jnp.bfloat16), grad_heads, preferred_element_type=jnp.float32
    )
    return (query_part, key_part, value_part)


def shards(
    frames,
    clip_lengths,
    text_states,
    text_segments,
    gain_one,
    shift_one,
    gain_two,
    shift_two,
    gain_three,
    shift_three,
    query_weight,
    key_weight,
    value_weight,
    output_weight,
    cross_query,
    cross_key,
    cross_value,
    cross_output,
    inner_weight,
    outer_weight,
    cotangent,
):
    row_count = frames.shape[0]
    text_count = text_states.shape[0]
    width_here = query_weight.shape[1]
    heads_here = width_here // HEAD_DIM
    blk_count = lax.axis_size("blk")
    blk_index = lax.axis_index("blk")
    scale = float(HEAD_DIM) ** (-0.5)
    my_first_row = blk_index * row_count
    offsets = jnp.arange(row_count, dtype=jnp.int32)
    rows = my_first_row + offsets
    segment, first = clip_rows(rows, clip_lengths)
    inputs = frames.astype(jnp.float32)
    normed_one = layer_norm(inputs, gain_one, shift_one).astype(jnp.bfloat16)
    queries = (matmul(normed_one, query_weight) * scale).astype(jnp.bfloat16)
    keys = matmul(normed_one, key_weight).astype(jnp.bfloat16)
    values = matmul(normed_one, value_weight).astype(jnp.bfloat16)
    query_heads = queries.reshape(row_count, heads_here, HEAD_DIM)
    start_state = (
        jnp.zeros((row_count, heads_here, HEAD_DIM), jnp.float32),
        jnp.full((heads_here, row_count), NEGATIVE, jnp.float32),
        jnp.zeros((heads_here, row_count), jnp.float32),
    )
    start = jnp.int32(0)
    key_piece = lax.all_gather(keys, "blk", axis=0, tiled=True)
    value_piece = lax.all_gather(values, "blk", axis=0, tiled=True)
    count = key_piece.shape[0]
    key_rows = jnp.arange(count, dtype=jnp.int32)

    def fold_work(state):
        totals, run_max, run_sum = state
        piece_keys = key_piece.reshape(count, heads_here, HEAD_DIM)
        piece_values = value_piece.reshape(count, heads_here, HEAD_DIM)
        score = jnp.einsum(
            "qhd,khd->hqk", query_heads, piece_keys, preferred_element_type=jnp.float32
        )
        allowed = (key_rows[None, :] <= rows[:, None]) & (key_rows[None, :] >= first[:, None])
        masked = jnp.where(allowed[None], score, NEGATIVE)
        new_max = jnp.maximum(run_max, jnp.max(masked, axis=-1))
        expo = jnp.where(allowed[None], jnp.exp(masked - new_max[:, :, None]), 0.0)
        run_sum = jnp.sum(expo, axis=-1)
        added = jnp.einsum(
            "hqk,khd->qhd",
            expo.astype(jnp.bfloat16),
            piece_values,
            preferred_element_type=jnp.float32,
        )
        totals = added
        return (totals, new_max, run_sum)

    needed = (start <= rows[-1]) & (start + count - 1 >= first[0])
    totals, run_max, run_sum = lax.cond(needed, fold_work, unchanged, start_state)
    self_out = totals / jnp.transpose(run_sum)[:, :, None]
    log_total = run_max + jnp.log(run_sum)
    attended = self_out.reshape(row_count, width_here).astype(jnp.bfloat16)
    first_sum = inputs + head_sum(matmul(attended, output_weight))
    normed_two = layer_norm(first_sum, gain_two, shift_two).astype(jnp.bfloat16)
    cross_queries = (matmul(normed_two, cross_query) * scale).astype(jnp.bfloat16)
    text_keys = matmul(text_states, cross_key).astype(jnp.bfloat16)
    text_values = matmul(text_states, cross_value).astype(jnp.bfloat16)
    cross_heads = cross_queries.reshape(row_count, heads_here, HEAD_DIM)
    text_key_heads = text_keys.reshape(text_count, heads_here, HEAD_DIM)
    text_value_heads = text_values.reshape(text_count, heads_here, HEAD_DIM)
    allowed_text = segment[:, None] == text_segments[None, :]
    cross_score = jnp.einsum(
        "qhd,khd->hqk", cross_heads, text_key_heads, preferred_element_type=jnp.float32
    )
    cross_masked = jnp.where(allowed_text[None], cross_score, NEGATIVE)
    cross_max = jnp.max(cross_masked, axis=-1, keepdims=True)
    cross_expo = jnp.where(allowed_text[None], jnp.exp(cross_masked - cross_max), 0.0)
    cross_weights = cross_expo / jnp.sum(cross_expo, axis=-1, keepdims=True)
    cross_weights_low = cross_weights.astype(jnp.bfloat16)
    cross_out = jnp.einsum(
        "hqk,khd->qhd", cross_weights_low, text_value_heads, preferred_element_type=jnp.float32
    )
    crossed = cross_out.reshape(row_count, width_here).astype(jnp.bfloat16)
    second_sum = first_sum + head_sum(matmul(crossed, cross_output))
    normed_three = layer_norm(second_sum, gain_three, shift_three).astype(jnp.bfloat16)
    hidden_pre = matmul(normed_three, inner_weight)
    hidden = gelu_exact(hidden_pre).astype(jnp.bfloat16)
    output = second_sum + head_sum(matmul(hidden, outer_weight))
    grad_output = cotangent.astype(jnp.float32)
    grad_outer = matmul(hidden.T, cotangent)
    grad_hidden = matmul(cotangent, outer_weight.T)
    _, gelu_back = jax.vjp(gelu_exact, hidden_pre)
    grad_pre = gelu_back(grad_hidden)[0].astype(jnp.bfloat16)
    grad_inner = matmul(normed_three.T, grad_pre)
    grad_normed_three = head_sum(matmul(grad_pre, inner_weight.T))
    through_three, grad_gain_three, grad_shift_three = norm_grads(
        second_sum, gain_three, shift_three, grad_normed_three
    )
    grad_second = grad_output + through_three
    grad_second_low = grad_second.astype(jnp.bfloat16)
    grad_cross_output = matmul(crossed.T, grad_second_low)
    grad_crossed = (
        matmul(grad_second_low, cross_output.T)
        .astype(jnp.bfloat16)
        .reshape(row_count, heads_here, HEAD_DIM)
    )
    grad_cross_weights = jnp.einsum(
        "qhd,khd->hqk", grad_crossed, text_value_heads, preferred_element_type=jnp.float32
    )
    cross_delta = jnp.transpose(jnp.sum(grad_crossed.astype(jnp.float32) * cross_out, axis=-1))
    grad_cross_score = (cross_weights * (grad_cross_weights - cross_delta[:, :, None])).astype(
        jnp.bfloat16
    )
    grad_cross_heads = jnp.einsum(
        "hqk,khd->qhd", grad_cross_score, text_key_heads, preferred_element_type=jnp.float32
    ).astype(jnp.bfloat16)
    grad_cross_queries = (grad_cross_heads * scale).reshape(row_count, width_here)
    text_key_part = jnp.einsum(
        "hqk,qhd->khd", grad_cross_score, cross_heads, preferred_element_type=jnp.float32
    )
    text_value_part = jnp.einsum(
        "hqk,qhd->khd", cross_weights_low, grad_crossed, preferred_element_type=jnp.float32
    )
    grad_text_keys, grad_text_values = lax.psum(
        (
            text_key_part.reshape(text_count, width_here),
            text_value_part.reshape(text_count, width_here),
        ),
        "blk",
    )
    grad_text_keys = grad_text_keys.astype(jnp.bfloat16)
    grad_text_values = grad_text_values.astype(jnp.bfloat16)
    grad_cross_key = matmul(text_states.T, grad_text_keys)
    grad_cross_value = matmul(text_states.T, grad_text_values)
    grad_text = lax.psum(
        (matmul(grad_text_keys, cross_key.T) + matmul(grad_text_values, cross_value.T)).astype(
            jnp.bfloat16
        ),
        "tp",
    ).astype(jnp.float32)
    grad_cross_query = matmul(normed_two.T, grad_cross_queries)
    grad_normed_two = head_sum(matmul(grad_cross_queries, cross_query.T))
    through_two, grad_gain_two, grad_shift_two = norm_grads(
        first_sum, gain_two, shift_two, grad_normed_two
    )
    grad_first = grad_second + through_two
    grad_first_low = grad_first.astype(jnp.bfloat16)
    grad_output_weight = matmul(attended.T, grad_first_low)
    grad_attended = matmul(grad_first_low, output_weight.T).astype(jnp.bfloat16)
    grad_heads = grad_attended.reshape(row_count, heads_here, HEAD_DIM)
    self_delta = jnp.transpose(jnp.sum(grad_heads.astype(jnp.float32) * self_out, axis=-1))
    zero_block = jnp.zeros((row_count, width_here), jnp.float32)

    def key_turn(turn, carry):
        source = (blk_index - turn) % blk_count
        base = source * row_count

        def key_work(state):
            key_block, value_block, key_grad, value_grad, query_grad = state
            query_part, key_part, value_part = block_grads(
                query_heads,
                grad_heads,
                log_total,
                self_delta,
                rows,
                first,
                key_block.reshape(row_count, heads_here, HEAD_DIM),
                value_block.reshape(row_count, heads_here, HEAD_DIM),
                base + offsets,
            )
            return (
                key_block,
                value_block,
                key_grad + key_part.reshape(row_count, width_here),
                value_grad + value_part.reshape(row_count, width_here),
                query_grad + query_part.reshape(row_count, width_here),
            )

        needed = (base <= rows[-1]) & (base + row_count - 1 >= first[0])
        key_block, value_block, key_grad, value_grad, query_grad = lax.cond(
            needed, key_work, unchanged, carry
        )
        key_block, value_block = shifted((key_block, value_block), "blk", 1)
        key_grad, value_grad = (
            shifted_2(key_grad.astype(jnp.bfloat16), "blk", 1).astype(key_grad.dtype),
            shifted_2(value_grad.astype(jnp.bfloat16), "blk", 1).astype(value_grad.dtype),
        )
        return (key_block, value_block, key_grad, value_grad, query_grad)

    final = lax.fori_loop(
        0, blk_count, key_turn, (keys, values, zero_block, zero_block, zero_block)
    )
    key_total, value_total, query_total = (final[2], final[3], final[4])
    grad_queries = query_total.astype(jnp.bfloat16) * scale
    grad_keys = key_total.astype(jnp.bfloat16)
    grad_values = value_total.astype(jnp.bfloat16)
    grad_query_weight = matmul(normed_one.T, grad_queries)
    grad_key_weight = matmul(normed_one.T, grad_keys)
    grad_value_weight = matmul(normed_one.T, grad_values)
    grad_normed_one = head_sum(
        matmul(grad_queries, query_weight.T)
        + matmul(grad_keys, key_weight.T)
        + matmul(grad_values, value_weight.T)
    )
    through_one, grad_gain_one, grad_shift_one = norm_grads(
        inputs, gain_one, shift_one, grad_normed_one
    )
    grad_frames = (grad_first + through_one).astype(jnp.bfloat16)
    (
        grad_query_weight,
        grad_key_weight,
        grad_value_weight,
        grad_output_weight,
        grad_cross_query,
        grad_cross_output,
        grad_inner,
        grad_outer,
        grad_gain_one,
        grad_shift_one,
        grad_gain_two,
        grad_shift_two,
        grad_gain_three,
        grad_shift_three,
    ) = lax.psum(
        (
            grad_query_weight,
            grad_key_weight,
            grad_value_weight,
            grad_output_weight,
            grad_cross_query,
            grad_cross_output,
            grad_inner,
            grad_outer,
            grad_gain_one,
            grad_shift_one,
            grad_gain_two,
            grad_shift_two,
            grad_gain_three,
            grad_shift_three,
        ),
        "blk",
    )
    return (
        output.astype(jnp.bfloat16),
        grad_frames,
        grad_text,
        grad_gain_one,
        grad_shift_one,
        grad_gain_two,
        grad_shift_two,
        grad_gain_three,
        grad_shift_three,
        grad_query_weight,
        grad_key_weight,
        grad_value_weight,
        grad_output_weight,
        grad_cross_query,
        grad_cross_key,
        grad_cross_value,
        grad_cross_output,
        grad_inner,
        grad_outer,
    )


def solution(mesh):
    return jax.shard_map(
        shards,
        mesh=mesh,
        in_specs=(
            P("blk", None),
            P(),
            P(),
            P(),
            P(),
            P(),
            P(),
            P(),
            P(),
            P(),
            P(None, "tp"),
            P(None, "tp"),
            P(None, "tp"),
            P("tp", None),
            P(None, "tp"),
            P(None, "tp"),
            P(None, "tp"),
            P("tp", None),
            P(None, "tp"),
            P("tp", None),
            P("blk", None),
        ),
        out_specs=(
            P("blk", None),
            P("blk", None),
            P(),
            P(),
            P(),
            P(),
            P(),
            P(),
            P(),
            P(None, "tp"),
            P(None, "tp"),
            P(None, "tp"),
            P("tp", None),
            P(None, "tp"),
            P(None, "tp"),
            P(None, "tp"),
            P("tp", None),
            P(None, "tp"),
            P("tp", None),
        ),
        check_vma=False,
    )
```

profile of v0, /device:TPU:0, one launch (start us, length us, event | category | flops | bytes accessed | tf_op | source)
XLA Modules:
  0.0 1468.9 jit_solution(12834105977165518617)
XLA Ops:
  10.0 2.6 convolution_convert_fusion.9
  21.8 44.2 %all-gather.3.cloned.1.call-done = bf16[4096,512]{1,0:T(8,128)(2,1)} async-done(((bf16[256,512]{1,0:T(8,128)(2,1)}), bf16[4096,512]{1,0:T(8,128)(2,1)}) %all-gather.3.cloned.1.call-update) | async-done | bytes 4194320 | tf_op jit(solution)/shard_map/all_gather | solution.py:136
  66.1 51.8 %all-gather.5.cloned.1.call-done = bf16[4096,512]{1,0:T(8,128)(2,1)} async-done(((bf16[256,512]{1,0:T(8,128)(2,1)}), bf16[4096,512]{1,0:T(8,128)(2,1)}) %all-gather.5.cloned.1.call-update) | async-done | bytes 4194320 | tf_op jit(solution)/shard_map/all_gather | solution.py:137
  117.9 62.9 %conditional.2 = (f32[256,8,64]{0,2,1:T(8,128)S(1)}, f32[8,256]{1,0:T(8,128)}, f32[8,256]{1,0:T(8,128)}, f32[8,256]{1,0:T(8,128)S(1)}) conditional(s32[]{:T(128)} %bitcast.13, () %tuple.55, (s32[4096]{0:T(1024)S(1)}, s32[4096]{0:T(1024)S(1)}, s32[256]{0:T(256)}, s32[256]{0:T(256)}, bf16[4096,512]{1,0:T(8,128)(2,1)}, ...), branch_computations={%region_5.6_spmd, %region_6.9_spmd} | conditional | flops 2234513408 | bytes 130910240 | solution.py:163
  117.9 6.3 copy.81
  125.8 6.3 copy.80
  132.2 15.7 %select_reduce_fusion = (f32[8,256]{1,0:T(8,128)S(1)}, f32[8,256,4096]{2,1,0:T(8,128)}) fusion(pred[256,4096]{1,0:T(8,128)(4,1)S(1)} %compare_and_fusion, bf16[256,8,64]{0,2,1:T(8,128)(2,1)S(1)} %get-tuple-element.475, bf16[4096,8,64]{0,2,1:T(8,128)(2,1)} %bitcast.126), kind=kOutput, calls=%fused_computation.2 | convolution fusion | flops 1090516992 | bytes 39067648 | tf_op jit(solution)/shard_map/cond/branch_1_fun/qhd,khd->hqk/dot_general | solution.py:145
  148.4 15.5 %fusion.7 = f32[256,8,64]{0,2,1:T(8,128)S(1)} fusion(bf16[4096,8,64]{0,2,1:T(8,128)(2,1)} %bitcast.133, f32[8,256,4096]{2,1,0:T(8,128)} %get-tuple-element.768, f32[8,256]{1,0:T(8,128)} %broadcast_maximum_fusion, pred[256,4096]{1,0:T(8,128)(4,1)S(1)} %compare_and_fusion), kind=kOutput, calls=%fused_computation.8 | convolution fusion | flops 1107296256 | bytes 39329792 | tf_op jit(solution)/shard_map/cond/branch_1_fun/hqk,khd->qhd/dot_general | solution.py:153
  163.9 16.2 %fusion.2 = f32[8,256]{1,0:T(8,128)} fusion(f32[8,256,4096]{2,1,0:T(8,128)} %get-tuple-element.768, f32[8,256]{1,0:T(8,128)} %broadcast_maximum_fusion, pred[256,4096]{1,0:T(8,128)(4,1)S(1)} %compare_and_fusion), kind=kLoop, calls=%fused_computation.3 | loop fusion | flops 33552384 | bytes 34619392 | tf_op jit(solution)/shard_map/cond/branch_1_fun/reduce_sum | solution.py:152
  181.7 2.6 convolution_convert_fusion.2
  189.6 21.9 %all-reduce.12.cloned.1.call-done = bf16[256,1024]{1,0:T(8,128)(2,1)} async-done(((bf16[256,1024]{1,0:T(8,128)(2,1)}), bf16[256,1024]{1,0:T(8,128)(2,1)}) %all-reduce.12.cloned.1.call-update) | async-done | bytes 524304 | tf_op jit(solution)/shard_map/psum | solution.py:51
  228.4 25.3 %all-reduce.14.cloned.1.call-done = bf16[256,1024]{1,0:T(8,128)(2,1)} async-done(((bf16[256,1024]{1,0:T(8,128)(2,1)}), bf16[256,1024]{1,0:T(8,128)(2,1)}) %all-reduce.14.cloned.1.call-update) | async-done | bytes 524304 | tf_op jit(solution)/shard_map/psum | solution.py:51
  256.5 3.7 fusion.86
  260.2 6.6 add_convert_fusion
  271.9 6.2 fusion.105
  280.3 4.8 fusion.85
  285.1 15.5 %all-reduce.16.cloned.1.call-done = bf16[256,1024]{1,0:T(8,128)(2,1)} async-done(((bf16[256,1024]{1,0:T(8,128)(2,1)}), bf16[256,1024]{1,0:T(8,128)(2,1)}) %all-reduce.16.cloned.1.call-update) | async-done | bytes 524304 | tf_op jit(solution)/shard_map/psum | solution.py:51
  317.8 25.6 %all-reduce.18.cloned.1.call-done = bf16[256,1024]{1,0:T(8,128)(2,1)} async-done(((bf16[256,1024]{1,0:T(8,128)(2,1)}), bf16[256,1024]{1,0:T(8,128)(2,1)}) %all-reduce.18.cloned.1.call-update) | async-done | bytes 524304 | tf_op jit(solution)/shard_map/psum | solution.py:51
  353.3 421.7 %while.26 = (s32[]{:T(128)}, bf16[256,512]{0,1:T(8,128)(2,1)S(1)}, bf16[256,512]{0,1:T(8,128)(2,1)}, f32[256,512]{0,1:T(8,128)}, f32[256,512]{0,1:T(8,128)}, /*i...) while((s32[]{:T(128)}, bf16[256,512]{0,1:T(8,128)(2,1)S(1)}, ...), condition=%wide.region_29.30_spmd.clone, body=%wide.region_26.29_spmd.clone.sunk | while | flops 341115168 | bytes 37714808 | solution.py:294
  359.2 5.0 conditional.5
  368.5 3.5 collective-permute-start.1
  384.2 6.3 collective-permute-start.2
  395.5 4.4 collective-permute-start.1
  413.3 7.3 collective-permute-start.3
  422.6 5.2 collective-permute-start.1
  443.0 7.5 collective-permute-start
  450.5 5.2 collective-permute-start.1
  473.5 10.1 collective-permute-start.1
  501.4 5.2 collective-permute-start.1
  517.0 2.9 collective-permute-start.2
  525.6 5.2 collective-permute-start.1
  543.6 6.3 collective-permute-start.3
  549.9 3.6 collective-permute-start
  553.5 5.2 collective-permute-start.1
  573.9 7.4 collective-permute-start
  581.3 5.2 collective-permute-start.1
  601.8 2.6 collective-permute-start
  604.4 9.1 collective-permute-start.1
  623.9 2.7 collective-permute-start.2
  629.7 2.6 collective-permute-start
  632.3 5.2 collective-permute-start.1
  647.9 2.8 collective-permute-start.2
  653.8 2.6 collective-permute-start
  656.4 5.2 collective-permute-start.1
  674.5 5.3 collective-permute-start.3
  679.7 4.6 collective-permute-start
  684.3 5.2 collective-permute-start.1
  704.7 7.4 collective-permute-start
  712.2 5.2 collective-permute-start.1
  732.6 2.6 collective-permute-start
  735.2 8.1 collective-permute-start.1
  754.2 3.2 collective-permute-start.2
  760.5 2.6 collective-permute-start
  763.1 5.2 collective-permute-start.1
  779.8 2.9 fusion.104
  784.6 31.8 %all-reduce.20.cloned.1.call-done = bf16[256,1024]{1,0:T(8,128)(2,1)} async-done(((bf16[256,1024]{1,0:T(8,128)(2,1)}), bf16[256,1024]{1,0:T(8,128)(2,1)}) %all-reduce.20.cloned.1.call-update) | async-done | bytes 524304 | tf_op jit(solution)/shard_map/psum | solution.py:51
  820.2 67.9 %all-reduce.25 = (bf16[128,512]{0,1:T(8,128)(2,1)S(1)}, bf16[128,512]{0,1:T(8,128)(2,1)}, f32[1024]{0:T(1024)}, f32[1024]{0:T(1024)}, f32[1024]{0:T(1024)}, /*in...) all-reduce(f32[128,512]{0,1:T(8,128)S(1)} %bitcast.142, ...), channel_id=1, replica_groups=mesh['blk'=16,'tp'=2] {'blk'}, use_global_device_ids=true, to_apply=%region_33.34 | all-reduce | flops 137216 | bytes 835584 | tf_op jit(solution)/shard_map/psum | solution.py:228
  900.5 2.9 copy.94
  905.2 2.9 copy.95
  909.3 13.6 all-reduce.24.cloned.1.call-done
  926.7 512.8 %all-reduce.22.cloned.1.call-done = (f32[1024,512]{1,0:T(8,128)}, f32[1024,512]{1,0:T(8,128)}, f32[1024,512]{1,0:T(8,128)}, f32[512,1024]{1,0:T(8,128)}, f32[102...) async-done(((f32[1024,512]{1,0:T(8,128)}, f32[1024,512]{1,0:T(8,128)}, f32[1024,512]{1,0:T(8,128)}, f32[512,1024]{1,0:T(8,128)}, ...) | async-done | bytes 29360144 | tf_op jit(solution)/shard_map/psum | solution.py:328
  1439.5 3.2 copy.158
  1453.1 4.3 copy.164
  1458.7 3.4 copy.165
  (680 shorter events, 340.7 us)
Async XLA Ops:
  7.3 58.8 %all-gather.3.cloned.1.call-start = ((), (), s32[]{:S(2)}) async-start(), calls=%async_computation | async-start | bytes 4456448 | tf_op jit(solution)/shard_map/all_gather | solution.py:136
  12.7 105.2 %all-gather.5.cloned.1.call-start = ((), (), s32[]{:S(2)}) async-start(), calls=%async_computation.1 | async-start | bytes 4456448 | tf_op jit(solution)/shard_map/all_gather | solution.py:137
  14.0 197.5 %all-reduce.12.cloned.1.call-start = ((), (), s32[]{:S(2)}) async-start(), calls=%async_computation.2 | async-start | bytes 1048576 | tf_op jit(solution)/shard_map/psum | solution.py:51
  184.3 69.4 %all-reduce.14.cloned.1.call-start = ((), (), s32[]{:S(2)}) async-start(), calls=%async_computation.3 | async-start | bytes 1048576 | tf_op jit(solution)/shard_map/psum | solution.py:51
  224.9 75.7 %all-reduce.16.cloned.1.call-start = ((), (), s32[]{:S(2)}) async-start(), calls=%async_computation.4 | async-start | bytes 1048576 | tf_op jit(solution)/shard_map/psum | solution.py:51
  271.9 71.5 %all-reduce.18.cloned.1.call-start = ((), (), s32[]{:S(2)}) async-start(), calls=%async_computation.5 | async-start | bytes 1048576 | tf_op jit(solution)/shard_map/psum | solution.py:51
  314.6 501.9 %all-reduce.20.cloned.1.call-start = ((), (), s32[]{:S(2)}) async-start(), calls=%async_computation.6 | async-start | bytes 1048576 | tf_op jit(solution)/shard_map/psum | solution.py:51
  364.2 8.7 collective-permute-start.2
  365.0 10.6 collective-permute-start.3
  366.6 9.8 collective-permute-start
  368.5 7.9 collective-permute-start.1
  384.2 15.7 %collective-permute-start.2 = (bf16[256,512]{0,1:T(8,128)(2,1)S(1)}, bf16[256,512]{0,1:T(8,128)(2,1)}, u32[]{:S(2)}, u32[]{:S(2)}) collective-permute-start(bf16[256,512]{0,1:T(8,128)(2,1)S(1)} %convert_element_type.500), channel_id=1, source_target_pairs={{0,2},{2,4},{4,6},{6,8},{8,10},{10,12},{12,14},{14,16},{16,18},{18... | collective-permute-start | bytes 786440 | tf_op jit(solution)/shard_map/while/body/eval_jaxpr/ppermute | solution.py:19
  391.2 10.5 collective-permute-start.3
  393.6 8.9 collective-permute-start
  410.3 17.5 %collective-permute-start.2 = (bf16[256,512]{0,1:T(8,128)(2,1)S(1)}, bf16[256,512]{0,1:T(8,128)(2,1)}, u32[]{:S(2)}, u32[]{:S(2)}) collective-permute-start(bf16[256,512]{0,1:T(8,128)(2,1)S(1)} %convert_element_type.500), channel_id=1, source_target_pairs={{0,2},{2,4},{4,6},{6,8},{8,10},{10,12},{12,14},{14,16},{16,18},{18... | collective-permute-start | bytes 786440 | tf_op jit(solution)/shard_map/while/body/eval_jaxpr/ppermute | solution.py:19
  413.3 16.3 %collective-permute-start.3 = (bf16[256,512]{0,1:T(8,128)(2,1)}, bf16[256,512]{0,1:T(8,128)(2,1)S(1)}, u32[]{:S(2)}, u32[]{:S(2)}) collective-permute-start(bf16[256,512]{0,1:T(8,128)(2,1)} %convert_element_type.502), channel_id=1, source_target_pairs={{0,2},{2,4},{4,6},{6,8},{8,10},{10,12},{12,14},{14,16},{16,18},{18... | collective-permute-start | bytes 786440 | tf_op jit(solution)/shard_map/while/body/eval_jaxpr/ppermute | solution.py:19
  420.6 9.8 collective-permute-start
  422.6 7.8 collective-permute-start.1
  438.2 17.5 %collective-permute-start.2 = (bf16[256,512]{0,1:T(8,128)(2,1)S(1)}, bf16[256,512]{0,1:T(8,128)(2,1)}, u32[]{:S(2)}, u32[]{:S(2)}) collective-permute-start(bf16[256,512]{0,1:T(8,128)(2,1)S(1)} %convert_element_type.500), channel_id=1, source_target_pairs={{0,2},{2,4},{4,6},{6,8},{8,10},{10,12},{12,14},{14,16},{16,18},{18... | collective-permute-start | bytes 786440 | tf_op jit(solution)/shard_map/while/body/eval_jaxpr/ppermute | solution.py:19
  440.7 16.8 %collective-permute-start.3 = (bf16[256,512]{0,1:T(8,128)(2,1)}, bf16[256,512]{0,1:T(8,128)(2,1)S(1)}, u32[]{:S(2)}, u32[]{:S(2)}) collective-permute-start(bf16[256,512]{0,1:T(8,128)(2,1)} %convert_element_type.502), channel_id=1, source_target_pairs={{0,2},{2,4},{4,6},{6,8},{8,10},{10,12},{12,14},{14,16},{16,18},{18... | collective-permute-start | bytes 786440 | tf_op jit(solution)/shard_map/while/body/eval_jaxpr/ppermute | solution.py:19
  443.0 15.3 %collective-permute-start = (bf16[256,512]{0,1:T(8,128)(2,1)S(1)}, bf16[256,512]{0,1:T(8,128)(2,1)S(1)}, u32[]{:S(2)}, u32[]{:S(2)}) collective-permute-start(bf16[256,512]{0,1:T(8,128)(2,1)S(1)} %copy.126), channel_id=1, source_target_pairs={{0,2},{2,4},{4,6},{6,8},{8,10},{10,12},{12,14},{14,16},{16,18},{18... | collective-permute-start | bytes 786440 | tf_op jit(solution)/shard_map/while/body/eval_jaxpr/ppermute | solution.py:14
  466.1 17.5 %collective-permute-start.2 = (bf16[256,512]{0,1:T(8,128)(2,1)S(1)}, bf16[256,512]{0,1:T(8,128)(2,1)}, u32[]{:S(2)}, u32[]{:S(2)}) collective-permute-start(bf16[256,512]{0,1:T(8,128)(2,1)S(1)} %convert_element_type.500), channel_id=1, source_target_pairs={{0,2},{2,4},{4,6},{6,8},{8,10},{10,12},{12,14},{14,16},{16,18},{18... | collective-permute-start | bytes 786440 | tf_op jit(solution)/shard_map/while/body/eval_jaxpr/ppermute | solution.py:19
  468.6 16.8 %collective-permute-start.3 = (bf16[256,512]{0,1:T(8,128)(2,1)}, bf16[256,512]{0,1:T(8,128)(2,1)S(1)}, u32[]{:S(2)}, u32[]{:S(2)}) collective-permute-start(bf16[256,512]{0,1:T(8,128)(2,1)} %convert_element_type.502), channel_id=1, source_target_pairs={{0,2},{2,4},{4,6},{6,8},{8,10},{10,12},{12,14},{14,16},{16,18},{18... | collective-permute-start | bytes 786440 | tf_op jit(solution)/shard_map/while/body/eval_jaxpr/ppermute | solution.py:19
  470.9 15.3 %collective-permute-start = (bf16[256,512]{0,1:T(8,128)(2,1)S(1)}, bf16[256,512]{0,1:T(8,128)(2,1)S(1)}, u32[]{:S(2)}, u32[]{:S(2)}) collective-permute-start(bf16[256,512]{0,1:T(8,128)(2,1)S(1)} %copy.126), channel_id=1, source_target_pairs={{0,2},{2,4},{4,6},{6,8},{8,10},{10,12},{12,14},{14,16},{16,18},{18... | collective-permute-start | bytes 786440 | tf_op jit(solution)/shard_map/while/body/eval_jaxpr/ppermute | solution.py:14
  473.5 12.7 collective-permute-start.1
  494.0 12.5 collective-permute-start.2
  496.5 11.9 collective-permute-start.3
  498.8 10.4 collective-permute-start
  517.0 13.8 collective-permute-start.2
  520.6 11.9 collective-permute-start.3
  523.0 10.4 collective-permute-start
  541.2 17.5 %collective-permute-start.2 = (bf16[256,512]{0,1:T(8,128)(2,1)S(1)}, bf16[256,512]{0,1:T(8,128)(2,1)}, u32[]{:S(2)}, u32[]{:S(2)}) collective-permute-start(bf16[256,512]{0,1:T(8,128)(2,1)S(1)} %convert_element_type.500), channel_id=1, source_target_pairs={{0,2},{2,4},{4,6},{6,8},{8,10},{10,12},{12,14},{14,16},{16,18},{18... | collective-permute-start | bytes 786440 | tf_op jit(solution)/shard_map/while/body/eval_jaxpr/ppermute | solution.py:19
  543.6 16.8 %collective-permute-start.3 = (bf16[256,512]{0,1:T(8,128)(2,1)}, bf16[256,512]{0,1:T(8,128)(2,1)S(1)}, u32[]{:S(2)}, u32[]{:S(2)}) collective-permute-start(bf16[256,512]{0,1:T(8,128)(2,1)} %convert_element_type.502), channel_id=1, source_target_pairs={{0,2},{2,4},{4,6},{6,8},{8,10},{10,12},{12,14},{14,16},{16,18},{18... | collective-permute-start | bytes 786440 | tf_op jit(solution)/shard_map/while/body/eval_jaxpr/ppermute | solution.py:19
  549.9 11.4 collective-permute-start
  569.1 17.4 %collective-permute-start.2 = (bf16[256,512]{0,1:T(8,128)(2,1)S(1)}, bf16[256,512]{0,1:T(8,128)(2,1)}, u32[]{:S(2)}, u32[]{:S(2)}) collective-permute-start(bf16[256,512]{0,1:T(8,128)(2,1)S(1)} %convert_element_type.500), channel_id=1, source_target_pairs={{0,2},{2,4},{4,6},{6,8},{8,10},{10,12},{12,14},{14,16},{16,18},{18... | collective-permute-start | bytes 786440 | tf_op jit(solution)/shard_map/while/body/eval_jaxpr/ppermute | solution.py:19
  571.5 16.8 %collective-permute-start.3 = (bf16[256,512]{0,1:T(8,128)(2,1)}, bf16[256,512]{0,1:T(8,128)(2,1)S(1)}, u32[]{:S(2)}, u32[]{:S(2)}) collective-permute-start(bf16[256,512]{0,1:T(8,128)(2,1)} %convert_element_type.502), channel_id=1, source_target_pairs={{0,2},{2,4},{4,6},{6,8},{8,10},{10,12},{12,14},{14,16},{16,18},{18... | collective-permute-start | bytes 786440 | tf_op jit(solution)/shard_map/while/body/eval_jaxpr/ppermute | solution.py:19
  573.9 15.2 %collective-permute-start = (bf16[256,512]{0,1:T(8,128)(2,1)S(1)}, bf16[256,512]{0,1:T(8,128)(2,1)S(1)}, u32[]{:S(2)}, u32[]{:S(2)}) collective-permute-start(bf16[256,512]{0,1:T(8,128)(2,1)S(1)} %copy.126), channel_id=1, source_target_pairs={{0,2},{2,4},{4,6},{6,8},{8,10},{10,12},{12,14},{14,16},{16,18},{18... | collective-permute-start | bytes 786440 | tf_op jit(solution)/shard_map/while/body/eval_jaxpr/ppermute | solution.py:14
  597.0 16.5 %collective-permute-start.2 = (bf16[256,512]{0,1:T(8,128)(2,1)S(1)}, bf16[256,512]{0,1:T(8,128)(2,1)}, u32[]{:S(2)}, u32[]{:S(2)}) collective-permute-start(bf16[256,512]{0,1:T(8,128)(2,1)S(1)} %convert_element_type.500), channel_id=1, source_target_pairs={{0,2},{2,4},{4,6},{6,8},{8,10},{10,12},{12,14},{14,16},{16,18},{18... | collective-permute-start | bytes 786440 | tf_op jit(solution)/shard_map/while/body/eval_jaxpr/ppermute | solution.py:19
  599.4 15.9 %collective-permute-start.3 = (bf16[256,512]{0,1:T(8,128)(2,1)}, bf16[256,512]{0,1:T(8,128)(2,1)S(1)}, u32[]{:S(2)}, u32[]{:S(2)}) collective-permute-start(bf16[256,512]{0,1:T(8,128)(2,1)} %convert_element_type.502), channel_id=1, source_target_pairs={{0,2},{2,4},{4,6},{6,8},{8,10},{10,12},{12,14},{14,16},{16,18},{18... | collective-permute-start | bytes 786440 | tf_op jit(solution)/shard_map/while/body/eval_jaxpr/ppermute | solution.py:19
  601.8 14.3 collective-permute-start
  604.4 11.7 collective-permute-start.1
  623.9 13.6 collective-permute-start.2
  627.3 12.0 collective-permute-start.3
  629.7 10.4 collective-permute-start
  647.9 13.7 collective-permute-start.2
  651.4 12.7 collective-permute-start.3
  653.8 11.1 collective-permute-start
  656.4 8.5 collective-permute-start.1
  672.8 16.7 %collective-permute-start.2 = (bf16[256,512]{0,1:T(8,128)(2,1)S(1)}, bf16[256,512]{0,1:T(8,128)(2,1)}, u32[]{:S(2)}, u32[]{:S(2)}) collective-permute-start(bf16[256,512]{0,1:T(8,128)(2,1)S(1)} %convert_element_type.500), channel_id=1, source_target_pairs={{0,2},{2,4},{4,6},{6,8},{8,10},{10,12},{12,14},{14,16},{16,18},{18... | collective-permute-start | bytes 786440 | tf_op jit(solution)/shard_map/while/body/eval_jaxpr/ppermute | solution.py:19
  674.5 16.8 %collective-permute-start.3 = (bf16[256,512]{0,1:T(8,128)(2,1)}, bf16[256,512]{0,1:T(8,128)(2,1)S(1)}, u32[]{:S(2)}, u32[]{:S(2)}) collective-permute-start(bf16[256,512]{0,1:T(8,128)(2,1)} %convert_element_type.502), channel_id=1, source_target_pairs={{0,2},{2,4},{4,6},{6,8},{8,10},{10,12},{12,14},{14,16},{16,18},{18... | collective-permute-start | bytes 786440 | tf_op jit(solution)/shard_map/while/body/eval_jaxpr/ppermute | solution.py:19
  679.7 12.4 collective-permute-start
  699.9 17.4 %collective-permute-start.2 = (bf16[256,512]{0,1:T(8,128)(2,1)S(1)}, bf16[256,512]{0,1:T(8,128)(2,1)}, u32[]{:S(2)}, u32[]{:S(2)}) collective-permute-start(bf16[256,512]{0,1:T(8,128)(2,1)S(1)} %convert_element_type.500), channel_id=1, source_target_pairs={{0,2},{2,4},{4,6},{6,8},{8,10},{10,12},{12,14},{14,16},{16,18},{18... | collective-permute-start | bytes 786440 | tf_op jit(solution)/shard_map/while/body/eval_jaxpr/ppermute | solution.py:19
  702.4 16.8 %collective-permute-start.3 = (bf16[256,512]{0,1:T(8,128)(2,1)}, bf16[256,512]{0,1:T(8,128)(2,1)S(1)}, u32[]{:S(2)}, u32[]{:S(2)}) collective-permute-start(bf16[256,512]{0,1:T(8,128)(2,1)} %convert_element_type.502), channel_id=1, source_target_pairs={{0,2},{2,4},{4,6},{6,8},{8,10},{10,12},{12,14},{14,16},{16,18},{18... | collective-permute-start | bytes 786440 | tf_op jit(solution)/shard_map/while/body/eval_jaxpr/ppermute | solution.py:19
  704.7 15.2 %collective-permute-start = (bf16[256,512]{0,1:T(8,128)(2,1)S(1)}, bf16[256,512]{0,1:T(8,128)(2,1)S(1)}, u32[]{:S(2)}, u32[]{:S(2)}) collective-permute-start(bf16[256,512]{0,1:T(8,128)(2,1)S(1)} %copy.126), channel_id=1, source_target_pairs={{0,2},{2,4},{4,6},{6,8},{8,10},{10,12},{12,14},{14,16},{16,18},{18... | collective-permute-start | bytes 786440 | tf_op jit(solution)/shard_map/while/body/eval_jaxpr/ppermute | solution.py:14
  727.8 15.5 %collective-permute-start.2 = (bf16[256,512]{0,1:T(8,128)(2,1)S(1)}, bf16[256,512]{0,1:T(8,128)(2,1)}, u32[]{:S(2)}, u32[]{:S(2)}) collective-permute-start(bf16[256,512]{0,1:T(8,128)(2,1)S(1)} %convert_element_type.500), channel_id=1, source_target_pairs={{0,2},{2,4},{4,6},{6,8},{8,10},{10,12},{12,14},{14,16},{16,18},{18... | collective-permute-start | bytes 786440 | tf_op jit(solution)/shard_map/while/body/eval_jaxpr/ppermute | solution.py:19
  730.2 15.3 %collective-permute-start.3 = (bf16[256,512]{0,1:T(8,128)(2,1)}, bf16[256,512]{0,1:T(8,128)(2,1)S(1)}, u32[]{:S(2)}, u32[]{:S(2)}) collective-permute-start(bf16[256,512]{0,1:T(8,128)(2,1)} %convert_element_type.502), channel_id=1, source_target_pairs={{0,2},{2,4},{4,6},{6,8},{8,10},{10,12},{12,14},{14,16},{16,18},{18... | collective-permute-start | bytes 786440 | tf_op jit(solution)/shard_map/while/body/eval_jaxpr/ppermute | solution.py:19
  732.6 13.8 collective-permute-start
  735.2 11.2 collective-permute-start.1
  754.2 16.6 %collective-permute-start.2 = (bf16[256,512]{0,1:T(8,128)(2,1)S(1)}, bf16[256,512]{0,1:T(8,128)(2,1)}, u32[]{:S(2)}, u32[]{:S(2)}) collective-permute-start(bf16[256,512]{0,1:T(8,128)(2,1)S(1)} %convert_element_type.500), channel_id=1, source_target_pairs={{0,2},{2,4},{4,6},{6,8},{8,10},{10,12},{12,14},{14,16},{16,18},{18... | collective-permute-start | bytes 786440 | tf_op jit(solution)/shard_map/while/body/eval_jaxpr/ppermute | solution.py:19
  758.1 15.3 %collective-permute-start.3 = (bf16[256,512]{0,1:T(8,128)(2,1)}, bf16[256,512]{0,1:T(8,128)(2,1)S(1)}, u32[]{:S(2)}, u32[]{:S(2)}) collective-permute-start(bf16[256,512]{0,1:T(8,128)(2,1)} %convert_element_type.502), channel_id=1, source_target_pairs={{0,2},{2,4},{4,6},{6,8},{8,10},{10,12},{12,14},{14,16},{16,18},{18... | collective-permute-start | bytes 786440 | tf_op jit(solution)/shard_map/while/body/eval_jaxpr/ppermute | solution.py:19
  760.5 13.8 collective-permute-start
  763.1 11.2 collective-permute-start.1
  779.7 143.2 %all-reduce.24.cloned.1.call-start = ((), (), s32[]{:S(2)}) async-start(), calls=%async_computation.8 | async-start | bytes 1572864 | tf_op jit(solution)/shard_map/psum | solution.py:51
  891.9 547.5 %all-reduce.22.cloned.1.call-start = ((), (), s32[]{:S(2)}) async-start(), calls=%async_computation.7 | async-start | bytes 58720256 | tf_op jit(solution)/shard_map/psum | solution.py:328
  (154 other events, 1374.3 us)
Sparse Core Ops, SparseCore 0:
  12.8 53.2 all-gather.2
  68.8 49.0 all-gather.4
  184.4 27.0 all-reduce.11
  225.1 28.5 all-reduce.13
  272.0 28.5 all-reduce.15
  314.7 28.5 all-reduce.17
  779.8 36.5 all-reduce.19
  892.0 30.8 all-reduce.23
  929.9 509.5 all-reduce.21
where the time goes:
time: 1480 us; the launch traced here: 1470 us
  waiting for transfers between devices  749 us (51%)
  starting transfers between devices  234 us (16%)
  local copies, waits for them, and re-layouts  142 us (10%)
  other arithmetic  127 us (9%)
  matrix products  109 us (7%)
  blocking collectives  67.9 us (5%)
  loops' own time  23.5 us (2%)
  between operations  16.3 us (1%)
    psum x1, waiting for transfers between devices, shards(): lax.psum((grad_query_weight, grad_key_weight, grad_value_weight, grad_out...  513 us
    ppermute x32, starting transfers between devices, shifted(): return lax.ppermute(block, axis, route)  149 us
    psum x6, waiting for transfers between devices, head_sum(): return lax.psum(values.astype(jnp.bfloat16), 'tp').astype(jnp.float32)  134 us
    ppermute x32, starting transfers between devices, shifted_2(): lax.ppermute(value, axis, [(i, (i + by) % size) for i in range(size)])  83.7 us
    psum x1, blocking collectives, shards(): lax.psum((text_key_part.reshape(text_count, width_here), text_value_part....  67.9 us
    dot_general x30, matrix products, matmul(): return jnp.dot(left, right, preferred_element_type=jnp.float32)  67 us
    all_gather x1, waiting for transfers between devices, shards(): value_piece = lax.all_gather(values, 'blk', axis=0, tiled=True)  51.8 us
    all_gather x1, waiting for transfers between devices, shards(): key_piece = lax.all_gather(keys, 'blk', axis=0, tiled=True)  44.2 us
  transfers between devices with their start and end apart: 73, of which 15 were waited for; matrix products, arithmetic and copies ran while one was open for 7% of the time, Pallas kernels for 0%

commit v1 on v0

--- a/solution.py
+++ b/solution.py
@@ -6,6 +6,12 @@
 HEAD_DIM = 64
 EPSILON = 1e-05
 NEGATIVE = -1e30
+
+
+def form_cycles(obj):
+    val = lax.all_gather(obj, "tp")
+    v_next = jnp.sum(val, 0)
+    return v_next
 
 
 def shifted(block, axis, distance):
@@ -48,7 +54,7 @@
 
 
 def head_sum(values):
-    return lax.psum(values.astype(jnp.bfloat16), "tp").astype(jnp.float32)
+    return form_cycles(values.astype(jnp.bfloat16)).astype(jnp.float32)
 
 
 def unchanged(state):

time: 1480 us -> 1410 us (0.953)
  local copies, waits for them, and re-layouts: 142 us -> 115 us
  other arithmetic: 127 us -> 104 us
  waiting for transfers between devices: 749 us -> 728 us
    psum x6 -> x1, waiting for transfers between devices: 134 us -> 6.25 us  [shards(): lax.psum((matmul(grad_text_keys, cross_key.T) + matmul(grad_text_values,...]
    all_gather x0 -> x6, waiting for transfers between devices: none -> 94.6 us  [form_cycles(): val = lax.all_gather(obj, 'tp')]
    while x128 -> x32, local copies, waits for them, and re-layouts: 39.7 us -> 11.6 us
    convert_element_type x16, other arithmetic: 28.5 us -> 0.59 us  [key_turn(): shifted_2(key_grad.astype(jnp.bfloat16), 'blk', 1).astype(key_grad.dtype)]
    convert_element_type x16, other arithmetic: 13.3 us -> 28.4 us  [key_turn(): shifted_2(value_grad.astype(jnp.bfloat16), 'blk', 1)]
    unnamed x198 -> x202, local copies, waits for them, and re-layouts: 39 us -> 43.8 us
  transfers between devices with their start and end apart: 73 -> 74, of which waited for: 15 -> 19; matrix products, arithmetic and copies ran while one was open for 7% -> 7% of each run, Pallas kernels for 0% -> 0%
where the time goes in v1:
time: 1410 us; the launch traced here: 1400 us
  waiting for transfers between devices  728 us (52%)
  starting transfers between devices  236 us (17%)
  local copies, waits for them, and re-layouts  115 us (8%)
  matrix products  107 us (8%)
  other arithmetic  104 us (7%)
  blocking collectives  68.1 us (5%)
  loops' own time  22.6 us (2%)
  between operations  16.8 us (1%)
    psum x1, waiting for transfers between devices, shards(): lax.psum((grad_query_weight, grad_key_weight, grad_value_weight, grad_out...  516 us
    ppermute x32, starting transfers between devices, shifted(): return lax.ppermute(block, axis, route)  152 us
    all_gather x6, waiting for transfers between devices, form_cycles(): val = lax.all_gather(obj, 'tp')  94.6 us
    ppermute x32, starting transfers between devices, shifted_2(): lax.ppermute(value, axis, [(i, (i + by) % size) for i in range(size)])  83 us
    psum x1, blocking collectives, shards(): lax.psum((text_key_part.reshape(text_count, width_here), text_value_part....  68.1 us
    dot_general x30, matrix products, matmul(): return jnp.dot(left, right, preferred_element_type=jnp.float32)  65.8 us
    all_gather x1, waiting for transfers between devices, shards(): value_piece = lax.all_gather(values, 'blk', axis=0, tiled=True)  51.8 us
    all_gather x1, waiting for transfers between devices, shards(): key_piece = lax.all_gather(keys, 'blk', axis=0, tiled=True)  44.2 us
  transfers between devices with their start and end apart: 74, of which 19 were waited for; matrix products, arithmetic and copies ran while one was open for 7% of the time, Pallas kernels for 0%

profile of v1, /device:TPU:0, one launch (start us, length us, event | category | flops | bytes accessed | tf_op | source)
XLA Modules:
  0.0 1398.0 jit_solution(18143351048581168564)
XLA Ops:
  21.8 44.2 %all-gather.15.cloned.1.call-done = bf16[4096,512]{1,0:T(8,128)(2,1)} async-done(((bf16[256,512]{1,0:T(8,128)(2,1)}), bf16[4096,512]{1,0:T(8,128)(2,1)}) %all-gather.15.cloned.1.call-update) | async-done | bytes 4194320 | tf_op jit(solution)/shard_map/all_gather | solution.py:142
  66.1 51.8 %all-gather.17.cloned.1.call-done = bf16[4096,512]{1,0:T(8,128)(2,1)} async-done(((bf16[256,512]{1,0:T(8,128)(2,1)}), bf16[4096,512]{1,0:T(8,128)(2,1)}) %all-gather.17.cloned.1.call-update) | async-done | bytes 4194320 | tf_op jit(solution)/shard_map/all_gather | solution.py:143
  117.9 62.9 %conditional.2 = (f32[256,8,64]{0,2,1:T(8,128)S(1)}, f32[8,256]{1,0:T(8,128)}, f32[8,256]{1,0:T(8,128)}, f32[8,256]{1,0:T(8,128)S(1)}) conditional(s32[]{:T(128)} %bitcast.13, () %tuple.55, (s32[4096]{0:T(1024)S(1)}, s32[4096]{0:T(1024)S(1)}, s32[256]{0:T(256)}, s32[256]{0:T(256)}, bf16[4096,512]{1,0:T(8,128)(2,1)}, ...), branch_computations={%region_5.6_spmd, %region_6.9_spmd} | conditional | flops 2234513408 | bytes 130910240 | solution.py:169
  117.9 6.3 copy.81
  125.8 6.3 copy.80
  132.2 15.6 %select_reduce_fusion = (f32[8,256]{1,0:T(8,128)S(1)}, f32[8,256,4096]{2,1,0:T(8,128)}) fusion(pred[256,4096]{1,0:T(8,128)(4,1)S(1)} %compare_and_fusion, bf16[256,8,64]{0,2,1:T(8,128)(2,1)S(1)} %get-tuple-element.475, bf16[4096,8,64]{0,2,1:T(8,128)(2,1)} %bitcast.132), kind=kOutput, calls=%fused_computation.2 | convolution fusion | flops 1090516992 | bytes 39067648 | tf_op jit(solution)/shard_map/cond/branch_1_fun/qhd,khd->hqk/dot_general | solution.py:151
  148.4 15.5 %fusion.7 = f32[256,8,64]{0,2,1:T(8,128)S(1)} fusion(bf16[4096,8,64]{0,2,1:T(8,128)(2,1)} %bitcast.139, f32[8,256,4096]{2,1,0:T(8,128)} %get-tuple-element.766, f32[8,256]{1,0:T(8,128)} %broadcast_maximum_fusion, pred[256,4096]{1,0:T(8,128)(4,1)S(1)} %compare_and_fusion), kind=kOutput, calls=%fused_computation.8 | convolution fusion | flops 1107296256 | bytes 39329792 | tf_op jit(solution)/shard_map/cond/branch_1_fun/hqk,khd->qhd/dot_general | solution.py:159
  163.9 16.2 %fusion.2 = f32[8,256]{1,0:T(8,128)} fusion(f32[8,256,4096]{2,1,0:T(8,128)} %get-tuple-element.766, f32[8,256]{1,0:T(8,128)} %broadcast_maximum_fusion, pred[256,4096]{1,0:T(8,128)(4,1)S(1)} %compare_and_fusion), kind=kLoop, calls=%fused_computation.3 | loop fusion | flops 33552384 | bytes 34619392 | tf_op jit(solution)/shard_map/cond/branch_1_fun/reduce_sum | solution.py:158
  190.8 13.4 all-gather.19.cloned.1.call-done
  217.0 21.4 %all-gather.21.cloned.1.call-done = bf16[512,1024]{1,0:T(8,128)(2,1)} async-done(((bf16[256,1024]{1,0:T(8,128)(2,1)}), bf16[512,1024]{1,0:T(8,128)(2,1)}) %all-gather.21.cloned.1.call-update) | async-done | bytes 1048592 | tf_op jit(solution)/shard_map/all_gather | solution.py:12
  243.6 3.7 fusion.86
  247.3 7.0 add_convert_fusion
  267.7 6.1 fusion.85
  273.8 5.1 all-gather.25.cloned.1.call-done
  284.6 17.7 %all-gather.23.cloned.1.call-done = bf16[512,1024]{1,0:T(8,128)(2,1)} async-done(((bf16[256,1024]{1,0:T(8,128)(2,1)}), bf16[512,1024]{1,0:T(8,128)(2,1)}) %all-gather.23.cloned.1.call-update) | async-done | bytes 1048592 | tf_op jit(solution)/shard_map/all_gather | solution.py:12
  316.3 4.7 fusion.105
  325.8 11.7 all-gather.27.cloned.1.call-done
  344.6 374.5 %while.26 = (s32[]{:T(128)}, bf16[256,512]{0,1:T(8,128)(2,1)S(1)}, bf16[256,512]{0,1:T(8,128)(2,1)S(1)}, f32[256,512]{0,1:T(8,128)S(1)}, f32[256,512]{0,1:T(8,12...) while((s32[]{:T(128)}, bf16[256,512]{0,1:T(8,128)(2,1)S(1)}, ...), condition=%wide.region_29.30_spmd.clone, body=%wide.region_26.29_spmd.clone.sunk | while | flops 341115168 | bytes 29326032 | solution.py:300
  349.3 4.1 conditional.5
  357.1 3.5 collective-permute-start.1
  372.4 4.4 collective-permute-start.2
  381.2 4.4 collective-permute-start.1
  393.1 3.6 collective-permute-start.2
  396.7 6.5 collective-permute-start.3
  405.3 5.2 collective-permute-start.1
  423.2 7.0 collective-permute-start
  430.3 5.2 collective-permute-start.1
  447.9 3.2 collective-permute-start
  451.1 9.3 collective-permute-start.1
  472.9 3.2 collective-permute-start
  476.1 5.2 collective-permute-start.1
  493.8 3.2 collective-permute-start
  497.0 5.2 collective-permute-start.1
  512.2 4.4 collective-permute-start.3
  516.6 4.9 collective-permute-start
  521.6 5.2 collective-permute-start.1
  539.2 7.3 collective-permute-start
  546.5 5.2 collective-permute-start.1
  564.2 3.2 collective-permute-start
  567.4 7.5 collective-permute-start.1
  582.5 4.2 collective-permute-start.2
  589.2 3.2 collective-permute-start
  592.4 5.2 collective-permute-start.1
  610.0 3.2 collective-permute-start
  613.2 5.2 collective-permute-start.1
  631.1 6.7 collective-permute-start
  637.9 5.2 collective-permute-start.1
  655.5 7.3 collective-permute-start
  662.8 5.2 collective-permute-start.1
  680.5 3.2 collective-permute-start
  683.7 5.8 collective-permute-start.1
  689.8 2.9 collective-permute-done.3
  705.4 3.2 collective-permute-start
  708.6 5.2 collective-permute-start.1
  714.5 2.9 collective-permute-done.3
  730.5 25.3 %all-gather.29.cloned.1.call-done = bf16[512,1024]{1,0:T(8,128)(2,1)} async-done(((bf16[256,1024]{1,0:T(8,128)(2,1)}), bf16[512,1024]{1,0:T(8,128)(2,1)}) %all-gather.29.cloned.1.call-update) | async-done | bytes 1048592 | tf_op jit(solution)/shard_map/all_gather | solution.py:12
  759.0 68.1 %all-reduce.9 = (bf16[128,512]{0,1:T(8,128)(2,1)S(1)}, bf16[128,512]{0,1:T(8,128)(2,1)}, f32[1024]{0:T(1024)}, f32[1024]{0:T(1024)}, f32[1024]{0:T(1024)}, /*ind...) all-reduce(f32[128,512]{0,1:T(8,128)S(1)} %bitcast.154, ...), channel_id=1, replica_groups=mesh['blk'=16,'tp'=2] {'blk'}, use_global_device_ids=true, to_apply=%region_33.34 | all-reduce | flops 137216 | bytes 835584 | tf_op jit(solution)/shard_map/psum | solution.py:234
  835.7 2.9 copy.94
  840.3 2.9 copy.95
  844.4 6.3 all-reduce.6.cloned.1.call-done
  852.5 515.6 %all-reduce.8.cloned.1.call-done = (f32[1024,512]{1,0:T(8,128)}, f32[1024,512]{1,0:T(8,128)}, f32[1024,512]{1,0:T(8,128)}, f32[512,1024]{1,0:T(8,128)}, f32[1024...) async-done(((f32[1024,512]{1,0:T(8,128)}, f32[1024,512]{1,0:T(8,128)}, f32[1024,512]{1,0:T(8,128)}, f32[512,1024]{1,0:T(8,128)}, ...) | async-done | bytes 29360144 | tf_op jit(solution)/shard_map/psum | solution.py:334
  1368.0 3.2 copy.152
  1381.6 4.3 copy.158
  1387.3 3.4 copy.159
  (590 shorter events, 305.1 us)
Async XLA Ops:
  7.3 58.8 %all-gather.15.cloned.1.call-start = ((), (), s32[]{:S(2)}) async-start(), calls=%async_computation | async-start | bytes 4456448 | tf_op jit(solution)/shard_map/all_gather | solution.py:142
  12.7 105.2 %all-gather.17.cloned.1.call-start = ((), (), s32[]{:S(2)}) async-start(), calls=%async_computation.1 | async-start | bytes 4456448 | tf_op jit(solution)/shard_map/all_gather | solution.py:143
  14.0 190.2 %all-gather.19.cloned.1.call-start = ((), (), s32[]{:S(2)}) async-start(), calls=%async_computation.3 | async-start | bytes 1572864 | tf_op jit(solution)/shard_map/all_gather | solution.py:12
  184.2 54.2 %all-gather.21.cloned.1.call-start = ((), (), s32[]{:S(2)}) async-start(), calls=%async_computation.4 | async-start | bytes 1572864 | tf_op jit(solution)/shard_map/all_gather | solution.py:12
  217.0 61.9 %all-gather.25.cloned.1.call-start = ((), (), s32[]{:S(2)}) async-start(), calls=%async_computation.6 | async-start | bytes 1572864 | tf_op jit(solution)/shard_map/all_gather | solution.py:12
  257.5 44.8 %all-gather.23.cloned.1.call-start = ((), (), s32[]{:S(2)}) async-start(), calls=%async_computation.5 | async-start | bytes 1572864 | tf_op jit(solution)/shard_map/all_gather | solution.py:12
  263.3 74.1 %all-gather.27.cloned.1.call-start = ((), (), s32[]{:S(2)}) async-start(), calls=%async_computation.7 | async-start | bytes 1572864 | tf_op jit(solution)/shard_map/all_gather | solution.py:12
  316.0 439.8 %all-gather.29.cloned.1.call-start = ((), (), s32[]{:S(2)}) async-start(), calls=%async_computation.8 | async-start | bytes 1572864 | tf_op jit(solution)/shard_map/all_gather | solution.py:12
  353.4 8.5 collective-permute-start.2
  353.5 11.4 collective-permute-start.3
  355.2 11.5 collective-permute-start
  357.1 9.6 collective-permute-start.1
  372.4 13.2 collective-permute-start.2
  376.8 8.8 collective-permute-start.3
  393.1 17.4 %collective-permute-start.2 = (bf16[256,512]{0,1:T(8,128)(2,1)S(1)}, bf16[256,512]{0,1:T(8,128)(2,1)S(1)}, u32[]{:S(2)}, u32[]{:S(2)}) collective-permute-start(bf16[256,512]{0,1:T(8,128)(2,1)S(1)} %convert_element_type.512), channel_id=1, source_target_pairs={{0,2},{2,4},{4,6},{6,8},{8,10},{10,12},{12,14},{14,16},{16,18},{18... | collective-permute-start | bytes 786440 | tf_op jit(solution)/shard_map/while/body/eval_jaxpr/ppermute | solution.py:25
  396.7 13.8 collective-permute-start.3
  403.3 9.1 collective-permute-start
  418.0 17.4 %collective-permute-start.2 = (bf16[256,512]{0,1:T(8,128)(2,1)S(1)}, bf16[256,512]{0,1:T(8,128)(2,1)S(1)}, u32[]{:S(2)}, u32[]{:S(2)}) collective-permute-start(bf16[256,512]{0,1:T(8,128)(2,1)S(1)} %convert_element_type.512), channel_id=1, source_target_pairs={{0,2},{2,4},{4,6},{6,8},{8,10},{10,12},{12,14},{14,16},{16,18},{18... | collective-permute-start | bytes 786440 | tf_op jit(solution)/shard_map/while/body/eval_jaxpr/ppermute | solution.py:25
  420.8 14.7 %collective-permute-start.3 = (bf16[256,512]{0,1:T(8,128)(2,1)S(1)}, bf16[256,512]{0,1:T(8,128)(2,1)}, u32[]{:S(2)}, u32[]{:S(2)}) collective-permute-start(bf16[256,512]{0,1:T(8,128)(2,1)S(1)} %convert_element_type.514), channel_id=1, source_target_pairs={{0,2},{2,4},{4,6},{6,8},{8,10},{10,12},{12,14},{14,16},{16,18},{18... | collective-permute-start | bytes 786440 | tf_op jit(solution)/shard_map/while/body/eval_jaxpr/ppermute | solution.py:25
  423.2 14.1 %collective-permute-start = (bf16[256,512]{0,1:T(8,128)(2,1)S(1)}, bf16[256,512]{0,1:T(8,128)(2,1)S(1)}, u32[]{:S(2)}, u32[]{:S(2)}) collective-permute-start(bf16[256,512]{0,1:T(8,128)(2,1)S(1)} %copy.122), channel_id=1, source_target_pairs={{0,2},{2,4},{4,6},{6,8},{8,10},{10,12},{12,14},{14,16},{16,18},{18... | collective-permute-start | bytes 786440 | tf_op jit(solution)/shard_map/while/body/eval_jaxpr/ppermute | solution.py:20
  443.0 17.4 %collective-permute-start.2 = (bf16[256,512]{0,1:T(8,128)(2,1)S(1)}, bf16[256,512]{0,1:T(8,128)(2,1)S(1)}, u32[]{:S(2)}, u32[]{:S(2)}) collective-permute-start(bf16[256,512]{0,1:T(8,128)(2,1)S(1)} %convert_element_type.512), channel_id=1, source_target_pairs={{0,2},{2,4},{4,6},{6,8},{8,10},{10,12},{12,14},{14,16},{16,18},{18... | collective-permute-start | bytes 786440 | tf_op jit(solution)/shard_map/while/body/eval_jaxpr/ppermute | solution.py:25
  445.5 15.0 %collective-permute-start.3 = (bf16[256,512]{0,1:T(8,128)(2,1)S(1)}, bf16[256,512]{0,1:T(8,128)(2,1)}, u32[]{:S(2)}, u32[]{:S(2)}) collective-permute-start(bf16[256,512]{0,1:T(8,128)(2,1)S(1)} %convert_element_type.514), channel_id=1, source_target_pairs={{0,2},{2,4},{4,6},{6,8},{8,10},{10,12},{12,14},{14,16},{16,18},{18... | collective-permute-start | bytes 786440 | tf_op jit(solution)/shard_map/while/body/eval_jaxpr/ppermute | solution.py:25
  447.9 14.3 %collective-permute-start = (bf16[256,512]{0,1:T(8,128)(2,1)S(1)}, bf16[256,512]{0,1:T(8,128)(2,1)S(1)}, u32[]{:S(2)}, u32[]{:S(2)}) collective-permute-start(bf16[256,512]{0,1:T(8,128)(2,1)S(1)} %copy.122), channel_id=1, source_target_pairs={{0,2},{2,4},{4,6},{6,8},{8,10},{10,12},{12,14},{14,16},{16,18},{18... | collective-permute-start | bytes 786440 | tf_op jit(solution)/shard_map/while/body/eval_jaxpr/ppermute | solution.py:20
  451.1 11.1 collective-permute-start.1
  468.0 13.3 collective-permute-start.2
  470.5 10.9 collective-permute-start.3
  472.9 10.2 collective-permute-start
  488.8 13.3 collective-permute-start.2
  491.3 10.9 collective-permute-start.3
  493.8 10.2 collective-permute-start
  509.7 17.1 %collective-permute-start.2 = (bf16[256,512]{0,1:T(8,128)(2,1)S(1)}, bf16[256,512]{0,1:T(8,128)(2,1)S(1)}, u32[]{:S(2)}, u32[]{:S(2)}) collective-permute-start(bf16[256,512]{0,1:T(8,128)(2,1)S(1)} %convert_element_type.512), channel_id=1, source_target_pairs={{0,2},{2,4},{4,6},{6,8},{8,10},{10,12},{12,14},{14,16},{16,18},{18... | collective-permute-start | bytes 786440 | tf_op jit(solution)/shard_map/while/body/eval_jaxpr/ppermute | solution.py:25
  512.2 14.6 %collective-permute-start.3 = (bf16[256,512]{0,1:T(8,128)(2,1)S(1)}, bf16[256,512]{0,1:T(8,128)(2,1)}, u32[]{:S(2)}, u32[]{:S(2)}) collective-permute-start(bf16[256,512]{0,1:T(8,128)(2,1)S(1)} %convert_element_type.514), channel_id=1, source_target_pairs={{0,2},{2,4},{4,6},{6,8},{8,10},{10,12},{12,14},{14,16},{16,18},{18... | collective-permute-start | bytes 786440 | tf_op jit(solution)/shard_map/while/body/eval_jaxpr/ppermute | solution.py:25
  516.6 12.0 collective-permute-start
  534.3 17.4 %collective-permute-start.2 = (bf16[256,512]{0,1:T(8,128)(2,1)S(1)}, bf16[256,512]{0,1:T(8,128)(2,1)S(1)}, u32[]{:S(2)}, u32[]{:S(2)}) collective-permute-start(bf16[256,512]{0,1:T(8,128)(2,1)S(1)} %convert_element_type.512), channel_id=1, source_target_pairs={{0,2},{2,4},{4,6},{6,8},{8,10},{10,12},{12,14},{14,16},{16,18},{18... | collective-permute-start | bytes 786440 | tf_op jit(solution)/shard_map/while/body/eval_jaxpr/ppermute | solution.py:25
  536.8 15.0 %collective-permute-start.3 = (bf16[256,512]{0,1:T(8,128)(2,1)S(1)}, bf16[256,512]{0,1:T(8,128)(2,1)}, u32[]{:S(2)}, u32[]{:S(2)}) collective-permute-start(bf16[256,512]{0,1:T(8,128)(2,1)S(1)} %convert_element_type.514), channel_id=1, source_target_pairs={{0,2},{2,4},{4,6},{6,8},{8,10},{10,12},{12,14},{14,16},{16,18},{18... | collective-permute-start | bytes 786440 | tf_op jit(solution)/shard_map/while/body/eval_jaxpr/ppermute | solution.py:25
  539.2 14.3 %collective-permute-start = (bf16[256,512]{0,1:T(8,128)(2,1)S(1)}, bf16[256,512]{0,1:T(8,128)(2,1)S(1)}, u32[]{:S(2)}, u32[]{:S(2)}) collective-permute-start(bf16[256,512]{0,1:T(8,128)(2,1)S(1)} %copy.122), channel_id=1, source_target_pairs={{0,2},{2,4},{4,6},{6,8},{8,10},{10,12},{12,14},{14,16},{16,18},{18... | collective-permute-start | bytes 786440 | tf_op jit(solution)/shard_map/while/body/eval_jaxpr/ppermute | solution.py:20
  559.3 15.7 %collective-permute-start.2 = (bf16[256,512]{0,1:T(8,128)(2,1)S(1)}, bf16[256,512]{0,1:T(8,128)(2,1)S(1)}, u32[]{:S(2)}, u32[]{:S(2)}) collective-permute-start(bf16[256,512]{0,1:T(8,128)(2,1)S(1)} %convert_element_type.512), channel_id=1, source_target_pairs={{0,2},{2,4},{4,6},{6,8},{8,10},{10,12},{12,14},{14,16},{16,18},{18... | collective-permute-start | bytes 786440 | tf_op jit(solution)/shard_map/while/body/eval_jaxpr/ppermute | solution.py:25
  561.8 13.2 collective-permute-start.3
  564.2 12.6 collective-permute-start
  567.4 9.4 collective-permute-start.1
  582.5 15.1 %collective-permute-start.2 = (bf16[256,512]{0,1:T(8,128)(2,1)S(1)}, bf16[256,512]{0,1:T(8,128)(2,1)S(1)}, u32[]{:S(2)}, u32[]{:S(2)}) collective-permute-start(bf16[256,512]{0,1:T(8,128)(2,1)S(1)} %convert_element_type.512), channel_id=1, source_target_pairs={{0,2},{2,4},{4,6},{6,8},{8,10},{10,12},{12,14},{14,16},{16,18},{18... | collective-permute-start | bytes 786440 | tf_op jit(solution)/shard_map/while/body/eval_jaxpr/ppermute | solution.py:25
  586.7 10.9 collective-permute-start.3
  589.2 10.2 collective-permute-start
  605.1 13.3 collective-permute-start.2
  607.6 12.9 collective-permute-start.3
  610.0 12.3 collective-permute-start
  613.2 9.1 collective-permute-start.1
  628.0 15.1 %collective-permute-start.2 = (bf16[256,512]{0,1:T(8,128)(2,1)S(1)}, bf16[256,512]{0,1:T(8,128)(2,1)S(1)}, u32[]{:S(2)}, u32[]{:S(2)}) collective-permute-start(bf16[256,512]{0,1:T(8,128)(2,1)S(1)} %convert_element_type.512), channel_id=1, source_target_pairs={{0,2},{2,4},{4,6},{6,8},{8,10},{10,12},{12,14},{14,16},{16,18},{18... | collective-permute-start | bytes 786440 | tf_op jit(solution)/shard_map/while/body/eval_jaxpr/ppermute | solution.py:25
  628.5 16.1 %collective-permute-start.3 = (bf16[256,512]{0,1:T(8,128)(2,1)S(1)}, bf16[256,512]{0,1:T(8,128)(2,1)}, u32[]{:S(2)}, u32[]{:S(2)}) collective-permute-start(bf16[256,512]{0,1:T(8,128)(2,1)S(1)} %convert_element_type.514), channel_id=1, source_target_pairs={{0,2},{2,4},{4,6},{6,8},{8,10},{10,12},{12,14},{14,16},{16,18},{18... | collective-permute-start | bytes 786440 | tf_op jit(solution)/shard_map/while/body/eval_jaxpr/ppermute | solution.py:25
  631.1 15.2 %collective-permute-start = (bf16[256,512]{0,1:T(8,128)(2,1)S(1)}, bf16[256,512]{0,1:T(8,128)(2,1)S(1)}, u32[]{:S(2)}, u32[]{:S(2)}) collective-permute-start(bf16[256,512]{0,1:T(8,128)(2,1)S(1)} %copy.122), channel_id=1, source_target_pairs={{0,2},{2,4},{4,6},{6,8},{8,10},{10,12},{12,14},{14,16},{16,18},{18... | collective-permute-start | bytes 786440 | tf_op jit(solution)/shard_map/while/body/eval_jaxpr/ppermute | solution.py:20
  637.9 8.5 collective-permute-start.1
  652.1 15.9 %collective-permute-start.2 = (bf16[256,512]{0,1:T(8,128)(2,1)S(1)}, bf16[256,512]{0,1:T(8,128)(2,1)S(1)}, u32[]{:S(2)}, u32[]{:S(2)}) collective-permute-start(bf16[256,512]{0,1:T(8,128)(2,1)S(1)} %convert_element_type.512), channel_id=1, source_target_pairs={{0,2},{2,4},{4,6},{6,8},{8,10},{10,12},{12,14},{14,16},{16,18},{18... | collective-permute-start | bytes 786440 | tf_op jit(solution)/shard_map/while/body/eval_jaxpr/ppermute | solution.py:25
  653.1 15.6 %collective-permute-start.3 = (bf16[256,512]{0,1:T(8,128)(2,1)S(1)}, bf16[256,512]{0,1:T(8,128)(2,1)}, u32[]{:S(2)}, u32[]{:S(2)}) collective-permute-start(bf16[256,512]{0,1:T(8,128)(2,1)S(1)} %convert_element_type.514), channel_id=1, source_target_pairs={{0,2},{2,4},{4,6},{6,8},{8,10},{10,12},{12,14},{14,16},{16,18},{18... | collective-permute-start | bytes 786440 | tf_op jit(solution)/shard_map/while/body/eval_jaxpr/ppermute | solution.py:25
  655.5 14.9 %collective-permute-start = (bf16[256,512]{0,1:T(8,128)(2,1)S(1)}, bf16[256,512]{0,1:T(8,128)(2,1)S(1)}, u32[]{:S(2)}, u32[]{:S(2)}) collective-permute-start(bf16[256,512]{0,1:T(8,128)(2,1)S(1)} %copy.122), channel_id=1, source_target_pairs={{0,2},{2,4},{4,6},{6,8},{8,10},{10,12},{12,14},{14,16},{16,18},{18... | collective-permute-start | bytes 786440 | tf_op jit(solution)/shard_map/while/body/eval_jaxpr/ppermute | solution.py:20
  676.1 13.7 collective-permute-start.2
  678.0 14.7 %collective-permute-start.3 = (bf16[256,512]{0,1:T(8,128)(2,1)S(1)}, bf16[256,512]{0,1:T(8,128)(2,1)}, u32[]{:S(2)}, u32[]{:S(2)}) collective-permute-start(bf16[256,512]{0,1:T(8,128)(2,1)S(1)} %convert_element_type.514), channel_id=1, source_target_pairs={{0,2},{2,4},{4,6},{6,8},{8,10},{10,12},{12,14},{14,16},{16,18},{18... | collective-permute-start | bytes 786440 | tf_op jit(solution)/shard_map/while/body/eval_jaxpr/ppermute | solution.py:25
  680.5 14.0 %collective-permute-start = (bf16[256,512]{0,1:T(8,128)(2,1)S(1)}, bf16[256,512]{0,1:T(8,128)(2,1)S(1)}, u32[]{:S(2)}, u32[]{:S(2)}) collective-permute-start(bf16[256,512]{0,1:T(8,128)(2,1)S(1)} %copy.122), channel_id=1, source_target_pairs={{0,2},{2,4},{4,6},{6,8},{8,10},{10,12},{12,14},{14,16},{16,18},{18... | collective-permute-start | bytes 786440 | tf_op jit(solution)/shard_map/while/body/eval_jaxpr/ppermute | solution.py:20
  683.7 10.8 collective-permute-start.1
  700.2 14.3 %collective-permute-start.2 = (bf16[256,512]{0,1:T(8,128)(2,1)S(1)}, bf16[256,512]{0,1:T(8,128)(2,1)S(1)}, u32[]{:S(2)}, u32[]{:S(2)}) collective-permute-start(bf16[256,512]{0,1:T(8,128)(2,1)S(1)} %convert_element_type.512), channel_id=1, source_target_pairs={{0,2},{2,4},{4,6},{6,8},{8,10},{10,12},{12,14},{14,16},{16,18},{18... | collective-permute-start | bytes 786440 | tf_op jit(solution)/shard_map/while/body/eval_jaxpr/ppermute | solution.py:25
  703.0 14.4 %collective-permute-start.3 = (bf16[256,512]{0,1:T(8,128)(2,1)S(1)}, bf16[256,512]{0,1:T(8,128)(2,1)}, u32[]{:S(2)}, u32[]{:S(2)}) collective-permute-start(bf16[256,512]{0,1:T(8,128)(2,1)S(1)} %convert_element_type.514), channel_id=1, source_target_pairs={{0,2},{2,4},{4,6},{6,8},{8,10},{10,12},{12,14},{14,16},{16,18},{18... | collective-permute-start | bytes 786440 | tf_op jit(solution)/shard_map/while/body/eval_jaxpr/ppermute | solution.py:25
  705.4 13.7 collective-permute-start
  708.6 10.5 collective-permute-start.1
  723.7 127.0 %all-reduce.6.cloned.1.call-start = ((), (), s32[]{:S(2)}) async-start(), calls=%async_computation.2 | async-start | bytes 524288 | tf_op jit(solution)/shard_map/psum | solution.py:245
  831.0 537.1 %all-reduce.8.cloned.1.call-start = ((), (), s32[]{:S(2)}) async-start(), calls=%async_computation.9 | async-start | bytes 58720256 | tf_op jit(solution)/shard_map/psum | solution.py:334
  (106 other events, 809.5 us)
Sparse Core Ops, SparseCore 0:
  12.8 53.2 all-gather.14
  68.8 49.0 all-gather.16
  184.3 19.7 all-gather.18
  217.1 21.2 all-gather.20
  257.6 21.2 all-gather.24
  280.9 21.2 all-gather.22
  316.1 21.2 all-gather.26
  723.8 31.9 all-gather.28
  831.1 19.5 all-reduce.5
  858.5 509.4 all-reduce.7
